TPU v7x, 32 devices: a whole 2x2x4 slice. The times are simulated.
32 devices in a mesh: ctx: 8 (over y, x, core), fsdp: 4 (over z).
Axes of the slice: x: 2, y: 2, z: 4, core: 2. Of those that a mesh axis runs over, the one named last changes fastest.
Arguments:
- tokens_in: bfloat16 [4, 1024, 1024], P('fsdp', 'ctx'), may hold values from -6 to 6
- doc_lengths: int32 [4, 8], P('fsdp'), may hold values from 1 to 512, 1024 in all within a row
- norm1_gain: bfloat16 [1024], P('fsdp'), may hold values from 0.5 to 1.5
- norm1_bias: bfloat16 [1024], P('fsdp'), may hold values from -1.5 to 1.5
- qkv_weight: bfloat16 [1024, 3072], P('fsdp'), may hold values from -0.1875 to 0.1875
- qv_bias: bfloat16 [2048], P('fsdp'), may hold values from -1.5 to 1.5
- out_weight: bfloat16 [1024, 1024], P('fsdp'), may hold values from -1.5 to 1.5
- out_bias: bfloat16 [1024], P('fsdp'), may hold values from -1.5 to 1.5
- norm2_gain: bfloat16 [1024], P('fsdp'), may hold values from 0.5 to 1.5
- norm2_bias: bfloat16 [1024], P('fsdp'), may hold values from -1.5 to 1.5
- up_weight: bfloat16 [1024, 4096], P('fsdp'), may hold values from -0.1875 to 0.1875
- up_bias: bfloat16 [4096], P('fsdp'), may hold values from -1.5 to 1.5
- down_weight: bfloat16 [4096, 1024], P('fsdp'), may hold values from -0.09375 to 0.09375
- down_bias: bfloat16 [1024], P('fsdp'), may hold values from -1.5 to 1.5
- out_cotangent: bfloat16 [4, 1024, 1024], P('fsdp', 'ctx'), may hold values from -6 to 6
Outputs:
- layer_out: bfloat16 [4, 1024, 1024], P('fsdp', 'ctx')
- input_grad: bfloat16 [4, 1024, 1024], P('fsdp', 'ctx')
- norm1_gain_grad: float32 [1024], P(('ctx', 'fsdp'))
- norm1_bias_grad: float32 [1024], P(('ctx', 'fsdp'))
- qkv_weight_grad: float32 [1024, 3072], P(('ctx', 'fsdp'))
- qv_bias_grad: float32 [2048], P(('ctx', 'fsdp'))
- out_weight_grad: float32 [1024, 1024], P(('ctx', 'fsdp'))
- out_bias_grad: float32 [1024], P(('ctx', 'fsdp'))
- norm2_gain_grad: float32 [1024], P(('ctx', 'fsdp'))
- norm2_bias_grad: float32 [1024], P(('ctx', 'fsdp'))
- up_weight_grad: float32 [1024, 4096], P(('ctx', 'fsdp'))
- up_bias_grad: float32 [4096], P(('ctx', 'fsdp'))
- down_weight_grad: float32 [4096, 1024], P(('ctx', 'fsdp'))
- down_bias_grad: float32 [1024], P(('ctx', 'fsdp'))
Inputs may be any that keep to these rules, and one draw needn't show every extreme that they name: `doc_lengths`: each row lists one stream's documents in order; they sum to 1024; the longest is 512.
All inputs are finite; a program needn't handle non-finite values.
Results may differ from a plain program's by a relative error of at most 0.018.
Values may be sent and summed in bfloat16 or wider, within the bound.
A program may use at most 128 MiB of HBM per device.

v0:
```python
import jax
import jax.numpy as jnp
from jax import lax
from jax.sharding import PartitionSpec as P

HEADS = 16
HEAD_DIM = 64
epsilon = 1e-05
masked_score = -1e30


def passed_along(block, axis, distance):
    devices = range(lax.axis_size(axis))
    route = [(i - distance, i) for i in devices if i - distance in devices]
    return lax.ppermute(block, axis, route)


def from_behind(x, axis, by):
    size = lax.axis_size(axis)
    return lax.ppermute(x, axis, [(i, (i + by) % size) for i in range(size)])


def norm_rows(values, gain, offset):
    centre = values - jnp.mean(values, axis=-1, keepdims=True)
    spread = jnp.mean(centre * centre, axis=-1, keepdims=True)
    return centre * lax.rsqrt(spread + epsilon) * gain + offset


def gelu_tanh(values):
    return jax.nn.gelu(values, approximate=True)


def doc_index(positions, doc_ends):
    return jnp.sum((doc_ends[None, :] <= positions[:, None]).astype(jnp.int32), axis=1)


def shards(
    tokens_in,
    doc_lengths,
    norm1_gain,
    norm1_bias,
    qkv_weight,
    qv_bias,
    out_weight,
    out_bias,
    norm2_gain,
    norm2_bias,
    up_weight,
    up_bias,
    down_weight,
    down_bias,
    out_cotangent,
):
    model_width = tokens_in.shape[2]
    tok_rows = tokens_in.shape[1]
    ctx_count = lax.axis_size("ctx")
    ctx_index = lax.axis_index("ctx")
    score_scale = HEAD_DIM ** (-0.5)
    inputs = tokens_in[0].astype(jnp.float32)
    doc_ends = jnp.cumsum(doc_lengths[0])
    query_pos = ctx_index * tok_rows + jnp.arange(tok_rows, dtype=jnp.int32)
    query_doc = doc_index(query_pos, doc_ends)

    def block_mask(anchor):
        key_pos = anchor * tok_rows + jnp.arange(tok_rows, dtype=jnp.int32)
        key_doc = doc_index(key_pos, doc_ends)
        return (key_pos[None, :] <= query_pos[:, None]) & (key_doc[None, :] == query_doc[:, None])

    attn_set = (
        lax.all_gather(norm1_gain, "fsdp", axis=0, tiled=True),
        lax.all_gather(norm1_bias, "fsdp", axis=0, tiled=True),
        lax.all_gather(qkv_weight, "fsdp", axis=0, tiled=True),
        lax.all_gather(qv_bias, "fsdp", axis=0, tiled=True),
        lax.all_gather(out_weight, "fsdp", axis=0, tiled=True),
        lax.all_gather(out_bias, "fsdp", axis=0, tiled=True),
    )
    gain_one, shift_one, w_qkv, b_qv, w_out, b_out = attn_set
    gain_one_f = gain_one.astype(jnp.float32)
    shift_one_f = shift_one.astype(jnp.float32)
    normed1 = norm_rows(inputs, gain_one_f, shift_one_f).astype(jnp.bfloat16)
    bias_full = jnp.concatenate(
        [b_qv[:model_width], jnp.zeros((model_width,), b_qv.dtype), b_qv[model_width:]]
    ).astype(jnp.float32)
    projected = (jnp.dot(normed1, w_qkv, preferred_element_type=jnp.float32) + bias_full).astype(
        jnp.bfloat16
    )
    queries = projected[:, :model_width].reshape(tok_rows, HEADS, HEAD_DIM)
    keys_own = projected[:, model_width : 2 * model_width].reshape(tok_rows, HEADS, HEAD_DIM)
    values_own = projected[:, 2 * model_width :].reshape(tok_rows, HEADS, HEAD_DIM)

    def attend(carry, keys, values, anchor):
        accum, running_top, running_total = carry
        allowed = block_mask(anchor)
        scores = (
            jnp.einsum("thd,shd->hts", queries, keys, preferred_element_type=jnp.float32)
            * score_scale
        )
        scores = jnp.where(allowed[None], scores, masked_score)
        new_top = jnp.maximum(running_top, jnp.max(scores, axis=2))
        weights = jnp.exp(scores - new_top[:, :, None])
        factor = jnp.exp(running_top - new_top)
        running_total = running_total * factor + jnp.sum(weights, axis=2)
        block_part = jnp.einsum(
            "hts,shd->thd", weights.astype(jnp.bfloat16), values, preferred_element_type=jnp.float32
        )
        accum = accum * factor.T[:, :, None] + block_part
        return (accum, new_top, running_total)

    start_carry = (
        jnp.zeros((tok_rows, HEADS, HEAD_DIM), jnp.float32),
        jnp.full((HEADS, tok_rows), masked_score, jnp.float32),
        jnp.zeros((HEADS, tok_rows), jnp.float32),
    )
    first_carry = attend(start_carry, keys_own, values_own, ctx_index)

    def cycle_forward(cycle_step, state):
        keys, values, carry = state
        keys, values = passed_along((keys, values), "ctx", 1)
        anchor = (ctx_index - cycle_step) % ctx_count
        return (keys, values, attend(carry, keys, values, anchor))

    _, _, final_carry = lax.fori_loop(
        1, ctx_count, cycle_forward, (keys_own, values_own, first_carry)
    )
    accum, running_top, running_total = final_carry
    log_total = running_top + jnp.log(running_total)
    mix = (accum / running_total.T[:, :, None]).reshape(tok_rows, model_width).astype(jnp.bfloat16)
    resid = (
        inputs + jnp.dot(mix, w_out, preferred_element_type=jnp.float32) + b_out.astype(jnp.float32)
    )
    mlp_set = (
        lax.all_gather(norm2_gain, "fsdp", axis=0, tiled=True),
        lax.all_gather(norm2_bias, "fsdp", axis=0, tiled=True),
        lax.all_gather(up_weight, "fsdp", axis=0, tiled=True),
        lax.all_gather(up_bias, "fsdp", axis=0, tiled=True),
        lax.all_gather(down_weight, "fsdp", axis=0, tiled=True),
        lax.all_gather(down_bias, "fsdp", axis=0, tiled=True),
    )
    gain_two, shift_two, w_up, b_up, w_down, b_down = mlp_set
    gain_two_f = gain_two.astype(jnp.float32)
    shift_two_f = shift_two.astype(jnp.float32)
    normed2 = norm_rows(resid, gain_two_f, shift_two_f).astype(jnp.bfloat16)
    pre = jnp.dot(normed2, w_up, preferred_element_type=jnp.float32) + b_up.astype(jnp.float32)
    hidden = gelu_tanh(pre).astype(jnp.bfloat16)
    result = (
        resid
        + jnp.dot(hidden, w_down, preferred_element_type=jnp.float32)
        + b_down.astype(jnp.float32)
    )
    layer_out = result.astype(jnp.bfloat16)[None]
    cotangent = out_cotangent[0]
    cotangent_f = cotangent.astype(jnp.float32)
    down_w_grad = jnp.einsum("tf,td->fd", hidden, cotangent, preferred_element_type=jnp.float32)
    down_b_grad = jnp.sum(cotangent_f, axis=0)
    hidden_grad = jnp.einsum("td,fd->tf", cotangent, w_down, preferred_element_type=jnp.float32)
    _, gelu_pull = jax.vjp(gelu_tanh, pre)
    pre_grad = gelu_pull(hidden_grad)[0].astype(jnp.bfloat16)
    up_w_grad = jnp.einsum("td,tf->df", normed2, pre_grad, preferred_element_type=jnp.float32)
    up_b_grad = jnp.sum(pre_grad.astype(jnp.float32), axis=0)
    normed2_grad = jnp.einsum("tf,df->td", pre_grad, w_up, preferred_element_type=jnp.float32)
    _, norm_two_pull = jax.vjp(norm_rows, resid, gain_two_f, shift_two_f)
    resid_part, gain_two_grad, shift_two_grad = norm_two_pull(normed2_grad)
    resid_grad = cotangent_f + resid_part
    mlp_sums = (
        lax.psum_scatter(gain_two_grad, ("ctx", "fsdp"), scatter_dimension=0, tiled=True),
        lax.psum_scatter(shift_two_grad, ("ctx", "fsdp"), scatter_dimension=0, tiled=True),
        lax.psum_scatter(up_w_grad, ("ctx", "fsdp"), scatter_dimension=0, tiled=True),
        lax.psum_scatter(up_b_grad, ("ctx", "fsdp"), scatter_dimension=0, tiled=True),
        lax.psum_scatter(down_w_grad, ("ctx", "fsdp"), scatter_dimension=0, tiled=True),
        lax.psum_scatter(down_b_grad, ("ctx", "fsdp"), scatter_dimension=0, tiled=True),
    )
    branch_grad = resid_grad.astype(jnp.bfloat16)
    out_w_grad = jnp.einsum("td,te->de", mix, branch_grad, preferred_element_type=jnp.float32)
    out_b_grad = jnp.sum(branch_grad.astype(jnp.float32), axis=0)
    mix_grad = jnp.einsum(
        "te,de->td", branch_grad, w_out, preferred_element_type=jnp.float32
    ).astype(jnp.bfloat16)
    mix_grad = mix_grad.reshape(tok_rows, HEADS, HEAD_DIM)
    delta = jnp.sum(
        mix_grad.astype(jnp.float32) * mix.reshape(tok_rows, HEADS, HEAD_DIM).astype(jnp.float32),
        axis=2,
    ).T

    def attend_back(query_grad, keys, values, key_grads, value_grads, anchor):
        allowed = block_mask(anchor)
        scores = (
            jnp.einsum("thd,shd->hts", queries, keys, preferred_element_type=jnp.float32)
            * score_scale
        )
        probs = jnp.where(allowed[None], jnp.exp(scores - log_total[:, :, None]), 0.0)
        value_grads = value_grads + jnp.einsum(
            "hts,thd->shd", probs.astype(jnp.bfloat16), mix_grad, preferred_element_type=jnp.float32
        )
        prob_grads = jnp.einsum(
            "thd,shd->hts", mix_grad, values, preferred_element_type=jnp.float32
        )
        score_grads = (probs * (prob_grads - delta[:, :, None])).astype(jnp.bfloat16)
        query_grad = query_grad + score_scale * jnp.einsum(
            "hts,shd->thd", score_grads, keys, preferred_element_type=jnp.float32
        )
        key_grads = key_grads + score_scale * jnp.einsum(
            "hts,thd->shd", score_grads, queries, preferred_element_type=jnp.float32
        )
        return (query_grad, key_grads, value_grads)

    def cycle_backward(cycle_step, state):
        keys, values, key_grads, value_grads, query_grad = state
        anchor = (ctx_index - cycle_step) % ctx_count
        query_grad, key_grads, value_grads = attend_back(
            query_grad, keys, values, key_grads, value_grads, anchor
        )
        keys, values, key_grads, value_grads = (
            from_behind(keys, "ctx", 1),
            from_behind(values, "ctx", 1),
            from_behind(key_grads.astype(jnp.bfloat16), "ctx", 1).astype(key_grads.dtype),
            from_behind(value_grads.astype(jnp.bfloat16), "ctx", 1).astype(value_grads.dtype),
        )
        return (keys, values, key_grads, value_grads, query_grad)

    zero_grads = jnp.zeros((tok_rows, HEADS, HEAD_DIM), jnp.float32)
    back_state = lax.fori_loop(
        0, ctx_count, cycle_backward, (keys_own, values_own, zero_grads, zero_grads, zero_grads)
    )
    key_grads = back_state[2]
    value_grads = back_state[3]
    query_grad = back_state[4]
    qkv_grad = jnp.concatenate(
        [
            query_grad.reshape(tok_rows, model_width),
            key_grads.reshape(tok_rows, model_width),
            value_grads.reshape(tok_rows, model_width),
        ],
        axis=1,
    ).astype(jnp.bfloat16)
    qkv_w_grad = jnp.einsum("td,te->de", normed1, qkv_grad, preferred_element_type=jnp.float32)
    column_sums = jnp.sum(qkv_grad.astype(jnp.float32), axis=0)
    qv_b_grad = jnp.concatenate([column_sums[:model_width], column_sums[2 * model_width :]])
    normed1_grad = jnp.einsum("te,de->td", qkv_grad, w_qkv, preferred_element_type=jnp.float32)
    _, norm_one_pull = jax.vjp(norm_rows, inputs, gain_one_f, shift_one_f)
    input_part, gain_one_grad, shift_one_grad = norm_one_pull(normed1_grad)
    input_grad = (resid_grad + input_part).astype(jnp.bfloat16)[None]
    attn_sums = (
        lax.psum_scatter(gain_one_grad, ("ctx", "fsdp"), scatter_dimension=0, tiled=True),
        lax.psum_scatter(shift_one_grad, ("ctx", "fsdp"), scatter_dimension=0, tiled=True),
        lax.psum_scatter(qkv_w_grad, ("ctx", "fsdp"), scatter_dimension=0, tiled=True),
        lax.psum_scatter(qv_b_grad, ("ctx", "fsdp"), scatter_dimension=0, tiled=True),
        lax.psum_scatter(out_w_grad, ("ctx", "fsdp"), scatter_dimension=0, tiled=True),
        lax.psum_scatter(out_b_grad, ("ctx", "fsdp"), scatter_dimension=0, tiled=True),
    )
    return (
        layer_out,
        input_grad,
        attn_sums[0],
        attn_sums[1],
        attn_sums[2],
        attn_sums[3],
        attn_sums[4],
        attn_sums[5],
        mlp_sums[0],
        mlp_sums[1],
        mlp_sums[2],
        mlp_sums[3],
        mlp_sums[4],
        mlp_sums[5],
    )


def solution(mesh):
    placed = (
        P("fsdp", "ctx", None),
        P("fsdp", None),
        P("fsdp"),
        P("fsdp"),
        P("fsdp", None),
        P("fsdp"),
        P("fsdp", None),
        P("fsdp"),
        P("fsdp"),
        P("fsdp"),
        P("fsdp", None),
        P("fsdp"),
        P("fsdp", None),
        P("fsdp"),
        P("fsdp", "ctx", None),
    )
    return jax.shard_map(
        shards,
        mesh=mesh,
        in_specs=placed,
        out_specs=(
            P("fsdp", "ctx", None),
            P("fsdp", "ctx", None),
            P(("ctx", "fsdp")),
            P(("ctx", "fsdp")),
            P(("ctx", "fsdp"), None),
            P(("ctx", "fsdp")),
            P(("ctx", "fsdp"), None),
            P(("ctx", "fsdp")),
            P(("ctx", "fsdp")),
            P(("ctx", "fsdp")),
            P(("ctx", "fsdp"), None),
            P(("ctx", "fsdp")),
            P(("ctx", "fsdp"), None),
            P(("ctx", "fsdp")),
        ),
        check_vma=False,
    )
```

profile of v0, /device:TPU:0, one launch (start us, length us, event | category | flops | bytes accessed | tf_op | source)
XLA Modules:
  0.0 1537.0 jit_solution(3058902817003224563)
XLA Ops:
  10.2 12.6 all-gather.3
  22.8 13.5 all-gather.2
  36.3 8.5 all-gather.1
  44.8 14.5 all-gather
  60.2 12.0 all_gather.45
  72.2 7.7 all-gather.5
  80.0 13.6 all-gather.4
  93.6 34.6 %all-gather.12.cloned.1.call-done = bf16[1024,3072]{1,0:T(8,128)(2,1)} async-done(((bf16[256,3072]{1,0:T(8,128)(2,1)}), bf16[1024,3072]{1,0:T(8,128)(2,1)}) %all-gather.12.cloned.1.call-update) | async-done | bytes 6291472 | tf_op jit(solution)/shard_map/all_gather | solution.py:72
  136.8 79.3 %while.48 = (s32[]{:T(128)}, bf16[128,16,64]{0,2,1:T(8,128)(2,1)S(1)}, bf16[128,16,64]{0,2,1:T(8,128)(2,1)}, f32[128,16,64]{0,2,1:T(8,128)S(1)}, f32[16,128]{1,0...) while((s32[]{:T(128)}, ...), condition=%wide.region_10.11_spmd.clone, body=%wide.region_6.0_spmd.clone.sunk | while | flops 69264528 | bytes 8294802 | solution.py:122
  144.8 4.9 collective-permute-start
  156.3 4.9 collective-permute-start
  167.8 4.9 collective-permute-start
  179.4 5.2 collective-permute-start
  191.2 5.8 collective-permute-start
  203.7 5.8 collective-permute-start
  218.6 105.3 %all-gather.16.cloned.1.call-done = bf16[1024,4096]{1,0:T(8,128)(2,1)} async-done(((bf16[256,4096]{1,0:T(8,128)(2,1)}), bf16[1024,4096]{1,0:T(8,128)(2,1)}) %all-gather.16.cloned.1.call-update) | async-done | bytes 8388624 | tf_op jit(solution)/shard_map/all_gather | solution.py:134
  323.8 6.1 convolution_add_fusion
  329.9 143.2 %all-gather.18.cloned.1.call-done = bf16[4096,1024]{1,0:T(8,128)(2,1)} async-done(((bf16[1024,1024]{1,0:T(8,128)(2,1)}), bf16[4096,1024]{1,0:T(8,128)(2,1)}) %all-gather.18.cloned.1.call-update) | async-done | bytes 8388624 | tf_op jit(solution)/shard_map/all_gather | solution.py:136
  473.2 7.8 convert_reduce_fusion.2
  490.8 145.1 %while.49 = (s32[]{:T(128)}, bf16[128,16,64]{0,2,1:T(8,128)(2,1)S(1)}, bf16[128,16,64]{0,2,1:T(8,128)(2,1)}, f32[128,16,64]{0,2,1:T(8,128)S(1)}, f32[128,16,64]{...) while((s32[]{:T(128)}, ...), condition=%wide.region_18.19_spmd.clone, body=%wide.region_16.18_spmd.clone.sunk | while | flops 171232400 | bytes 16044550 | solution.py:221
  499.7 4.9 collective-permute-done.4
  536.7 4.7 collective-permute-done.4
  637.1 6.4 fusion.66
  644.8 9.0 fusion.71
  654.8 10.7 fusion.56
  666.2 9.3 all-gather.6
  675.8 5.5 fusion.72
  682.7 43.7 %all-reduce.8 = (f32[1024]{0:T(1024)S(1)}, f32[1024]{0:T(1024)S(1)}, f32[2048]{0:T(1024)S(1)}, f32[1024]{0:T(1024)S(1)}, f32[1024]{0:T(1024)S(1)}, /*index=5*/f3...) all-reduce(f32[1024]{0:T(1024)S(1)} %get-tuple-element.720, ...), channel_id=2, replica_groups=mesh['ctx'=8,'fsdp'=4] {'ctx','fsdp'}, use_global_device_ids=true, to_apply=%region_22.23.clone | all-reduce | flops 12288 | bytes 98304
  731.1 6.5 fusion.37
  737.7 61.1 %reduce-scatter.5.cloned.1.call-done = f32[32,3072]{1,0:T(8,128)} async-done(((f32[1024,3072]{1,0:T(8,128)}), f32[32,3072]{1,0:T(8,128)}) %reduce-scatter.5.cloned.1.call-update) | async-done | bytes 393232 | tf_op jit(solution)/shard_map/reduce_scatter | solution.py:245
  798.7 366.3 %reduce-scatter.9.cloned.1.call-done = f32[32,4096]{1,0:T(8,128)} async-done(((f32[1024,4096]{1,0:T(8,128)}), f32[32,4096]{1,0:T(8,128)}) %reduce-scatter.9.cloned.1.call-update) | async-done | bytes 524304 | tf_op jit(solution)/shard_map/reduce_scatter | solution.py:167
  1165.0 365.1 %reduce-scatter.11.cloned.1.call-done = f32[128,1024]{1,0:T(8,128)} async-done(((f32[4096,1024]{1,0:T(8,128)}), f32[128,1024]{1,0:T(8,128)}) %reduce-scatter.11.cloned.1.call-update) | async-done | bytes 524304 | tf_op jit(solution)/shard_map/reduce_scatter | solution.py:169
  (401 shorter events, 216.4 us)
Async XLA Ops:
  7.2 121.0 %all-gather.12.cloned.1.call-start = ((), (), s32[]{:S(2)}) async-start(), calls=%async_computation.4 | async-start | bytes 7864320 | tf_op jit(solution)/shard_map/all_gather | solution.py:72
  7.9 208.3 %all-gather.14.cloned.1.call-start = ((), (), s32[]{:S(2)}) async-start(), calls=%async_computation.5 | async-start | bytes 2621440 | tf_op jit(solution)/shard_map/all_gather | solution.py:74
  8.8 315.1 %all-gather.16.cloned.1.call-start = ((), (), s32[]{:S(2)}) async-start(), calls=%async_computation.6 | async-start | bytes 10485760 | tf_op jit(solution)/shard_map/all_gather | solution.py:134
  9.5 463.7 %all-gather.18.cloned.1.call-start = ((), (), s32[]{:S(2)}) async-start(), calls=%async_computation.7 | async-start | bytes 10485760 | tf_op jit(solution)/shard_map/all_gather | solution.py:136
  10.1 727.6 %reduce-scatter.7.cloned.1.call-start = ((), (), s32[]{:S(2)}) async-start(), calls=%async_computation.9 | async-start | bytes 4325376 | tf_op jit(solution)/shard_map/reduce_scatter | solution.py:247
  490.8 308.0 %reduce-scatter.5.cloned.1.call-start = ((), (), s32[]{:S(2)}) async-start(), calls=%async_computation.8 | async-start | bytes 12976128 | tf_op jit(solution)/shard_map/reduce_scatter | solution.py:245
  491.1 17.7 %collective-permute-start.2 = (bf16[128,16,64]{0,2,1:T(8,128)(2,1)S(1)}, bf16[128,16,64]{0,2,1:T(8,128)(2,1)S(1)}, u32[]{:S(2)}, u32[]{:S(2)}) collective-permute-start(bf16[128,16,64]{0,2,1:T(8,128)(2,1)S(1)} %copy.89), channel_id=1, source_target_pairs={{0,4},{4,8},{8,12},{12,16},{16,20},{20,24},{24,28},{28,0},{1,5},{5... | collective-permute-start | bytes 786440 | tf_op jit(solution)/shard_map/while/body/eval_jaxpr/ppermute | solution.py:20
  492.1 16.6 %collective-permute-start.3 = (bf16[128,16,64]{0,2,1:T(8,128)(2,1)S(1)}, bf16[128,16,64]{0,2,1:T(8,128)(2,1)}, u32[]{:S(2)}, u32[]{:S(2)}) collective-permute-start(bf16[128,16,64]{0,2,1:T(8,128)(2,1)S(1)} %copy.90), channel_id=1, source_target_pairs={{0,4},{4,8},{8,12},{12,16},{16,20},{20,24},{24,28},{28,0},{1,5},{5... | collective-permute-start | bytes 786440 | tf_op jit(solution)/shard_map/while/body/eval_jaxpr/ppermute | solution.py:20
  508.8 18.3 %collective-permute-start.2 = (bf16[128,16,64]{0,2,1:T(8,128)(2,1)S(1)}, bf16[128,16,64]{0,2,1:T(8,128)(2,1)S(1)}, u32[]{:S(2)}, u32[]{:S(2)}) collective-permute-start(bf16[128,16,64]{0,2,1:T(8,128)(2,1)S(1)} %copy.89), channel_id=1, source_target_pairs={{0,4},{4,8},{8,12},{12,16},{16,20},{20,24},{24,28},{28,0},{1,5},{5... | collective-permute-start | bytes 786440 | tf_op jit(solution)/shard_map/while/body/eval_jaxpr/ppermute | solution.py:20
  509.8 17.3 %collective-permute-start.3 = (bf16[128,16,64]{0,2,1:T(8,128)(2,1)S(1)}, bf16[128,16,64]{0,2,1:T(8,128)(2,1)}, u32[]{:S(2)}, u32[]{:S(2)}) collective-permute-start(bf16[128,16,64]{0,2,1:T(8,128)(2,1)S(1)} %copy.90), channel_id=1, source_target_pairs={{0,4},{4,8},{8,12},{12,16},{16,20},{20,24},{24,28},{28,0},{1,5},{5... | collective-permute-start | bytes 786440 | tf_op jit(solution)/shard_map/while/body/eval_jaxpr/ppermute | solution.py:20
  513.7 12.4 collective-permute-start.5
  527.2 18.2 %collective-permute-start.2 = (bf16[128,16,64]{0,2,1:T(8,128)(2,1)S(1)}, bf16[128,16,64]{0,2,1:T(8,128)(2,1)S(1)}, u32[]{:S(2)}, u32[]{:S(2)}) collective-permute-start(bf16[128,16,64]{0,2,1:T(8,128)(2,1)S(1)} %copy.89), channel_id=1, source_target_pairs={{0,4},{4,8},{8,12},{12,16},{16,20},{20,24},{24,28},{28,0},{1,5},{5... | collective-permute-start | bytes 786440 | tf_op jit(solution)/shard_map/while/body/eval_jaxpr/ppermute | solution.py:20
  528.2 17.2 %collective-permute-start.3 = (bf16[128,16,64]{0,2,1:T(8,128)(2,1)S(1)}, bf16[128,16,64]{0,2,1:T(8,128)(2,1)}, u32[]{:S(2)}, u32[]{:S(2)}) collective-permute-start(bf16[128,16,64]{0,2,1:T(8,128)(2,1)S(1)} %copy.90), channel_id=1, source_target_pairs={{0,4},{4,8},{8,12},{12,16},{16,20},{20,24},{24,28},{28,0},{1,5},{5... | collective-permute-start | bytes 786440 | tf_op jit(solution)/shard_map/while/body/eval_jaxpr/ppermute | solution.py:20
  530.4 11.0 collective-permute-start.4
  531.4 13.0 collective-permute-start.5
  545.4 18.1 %collective-permute-start.2 = (bf16[128,16,64]{0,2,1:T(8,128)(2,1)S(1)}, bf16[128,16,64]{0,2,1:T(8,128)(2,1)S(1)}, u32[]{:S(2)}, u32[]{:S(2)}) collective-permute-start(bf16[128,16,64]{0,2,1:T(8,128)(2,1)S(1)} %copy.89), channel_id=1, source_target_pairs={{0,4},{4,8},{8,12},{12,16},{16,20},{20,24},{24,28},{28,0},{1,5},{5... | collective-permute-start | bytes 786440 | tf_op jit(solution)/shard_map/while/body/eval_jaxpr/ppermute | solution.py:20
  546.5 17.1 %collective-permute-start.3 = (bf16[128,16,64]{0,2,1:T(8,128)(2,1)S(1)}, bf16[128,16,64]{0,2,1:T(8,128)(2,1)}, u32[]{:S(2)}, u32[]{:S(2)}) collective-permute-start(bf16[128,16,64]{0,2,1:T(8,128)(2,1)S(1)} %copy.90), channel_id=1, source_target_pairs={{0,4},{4,8},{8,12},{12,16},{16,20},{20,24},{24,28},{28,0},{1,5},{5... | collective-permute-start | bytes 786440 | tf_op jit(solution)/shard_map/while/body/eval_jaxpr/ppermute | solution.py:20
  549.7 12.8 collective-permute-start.5
  563.6 18.0 %collective-permute-start.2 = (bf16[128,16,64]{0,2,1:T(8,128)(2,1)S(1)}, bf16[128,16,64]{0,2,1:T(8,128)(2,1)S(1)}, u32[]{:S(2)}, u32[]{:S(2)}) collective-permute-start(bf16[128,16,64]{0,2,1:T(8,128)(2,1)S(1)} %copy.89), channel_id=1, source_target_pairs={{0,4},{4,8},{8,12},{12,16},{16,20},{20,24},{24,28},{28,0},{1,5},{5... | collective-permute-start | bytes 786440 | tf_op jit(solution)/shard_map/while/body/eval_jaxpr/ppermute | solution.py:20
  564.6 17.0 %collective-permute-start.3 = (bf16[128,16,64]{0,2,1:T(8,128)(2,1)S(1)}, bf16[128,16,64]{0,2,1:T(8,128)(2,1)}, u32[]{:S(2)}, u32[]{:S(2)}) collective-permute-start(bf16[128,16,64]{0,2,1:T(8,128)(2,1)S(1)} %copy.90), channel_id=1, source_target_pairs={{0,4},{4,8},{8,12},{12,16},{16,20},{20,24},{24,28},{28,0},{1,5},{5... | collective-permute-start | bytes 786440 | tf_op jit(solution)/shard_map/while/body/eval_jaxpr/ppermute | solution.py:20
  567.8 12.8 collective-permute-start.5
  581.7 18.0 %collective-permute-start.2 = (bf16[128,16,64]{0,2,1:T(8,128)(2,1)S(1)}, bf16[128,16,64]{0,2,1:T(8,128)(2,1)S(1)}, u32[]{:S(2)}, u32[]{:S(2)}) collective-permute-start(bf16[128,16,64]{0,2,1:T(8,128)(2,1)S(1)} %copy.89), channel_id=1, source_target_pairs={{0,4},{4,8},{8,12},{12,16},{16,20},{20,24},{24,28},{28,0},{1,5},{5... | collective-permute-start | bytes 786440 | tf_op jit(solution)/shard_map/while/body/eval_jaxpr/ppermute | solution.py:20
  582.7 17.0 %collective-permute-start.3 = (bf16[128,16,64]{0,2,1:T(8,128)(2,1)S(1)}, bf16[128,16,64]{0,2,1:T(8,128)(2,1)}, u32[]{:S(2)}, u32[]{:S(2)}) collective-permute-start(bf16[128,16,64]{0,2,1:T(8,128)(2,1)S(1)} %copy.90), channel_id=1, source_target_pairs={{0,4},{4,8},{8,12},{12,16},{16,20},{20,24},{24,28},{28,0},{1,5},{5... | collective-permute-start | bytes 786440 | tf_op jit(solution)/shard_map/while/body/eval_jaxpr/ppermute | solution.py:20
  586.0 12.7 collective-permute-start.5
  599.8 18.0 %collective-permute-start.2 = (bf16[128,16,64]{0,2,1:T(8,128)(2,1)S(1)}, bf16[128,16,64]{0,2,1:T(8,128)(2,1)S(1)}, u32[]{:S(2)}, u32[]{:S(2)}) collective-permute-start(bf16[128,16,64]{0,2,1:T(8,128)(2,1)S(1)} %copy.89), channel_id=1, source_target_pairs={{0,4},{4,8},{8,12},{12,16},{16,20},{20,24},{24,28},{28,0},{1,5},{5... | collective-permute-start | bytes 786440 | tf_op jit(solution)/shard_map/while/body/eval_jaxpr/ppermute | solution.py:20
  600.8 17.0 %collective-permute-start.3 = (bf16[128,16,64]{0,2,1:T(8,128)(2,1)S(1)}, bf16[128,16,64]{0,2,1:T(8,128)(2,1)}, u32[]{:S(2)}, u32[]{:S(2)}) collective-permute-start(bf16[128,16,64]{0,2,1:T(8,128)(2,1)S(1)} %copy.90), channel_id=1, source_target_pairs={{0,4},{4,8},{8,12},{12,16},{16,20},{20,24},{24,28},{28,0},{1,5},{5... | collective-permute-start | bytes 786440 | tf_op jit(solution)/shard_map/while/body/eval_jaxpr/ppermute | solution.py:20
  604.5 12.3 collective-permute-start.5
  617.9 18.0 %collective-permute-start.2 = (bf16[128,16,64]{0,2,1:T(8,128)(2,1)S(1)}, bf16[128,16,64]{0,2,1:T(8,128)(2,1)S(1)}, u32[]{:S(2)}, u32[]{:S(2)}) collective-permute-start(bf16[128,16,64]{0,2,1:T(8,128)(2,1)S(1)} %copy.89), channel_id=1, source_target_pairs={{0,4},{4,8},{8,12},{12,16},{16,20},{20,24},{24,28},{28,0},{1,5},{5... | collective-permute-start | bytes 786440 | tf_op jit(solution)/shard_map/while/body/eval_jaxpr/ppermute | solution.py:20
  618.9 17.0 %collective-permute-start.3 = (bf16[128,16,64]{0,2,1:T(8,128)(2,1)S(1)}, bf16[128,16,64]{0,2,1:T(8,128)(2,1)}, u32[]{:S(2)}, u32[]{:S(2)}) collective-permute-start(bf16[128,16,64]{0,2,1:T(8,128)(2,1)S(1)} %copy.90), channel_id=1, source_target_pairs={{0,4},{4,8},{8,12},{12,16},{16,20},{20,24},{24,28},{28,0},{1,5},{5... | collective-permute-start | bytes 786440 | tf_op jit(solution)/shard_map/while/body/eval_jaxpr/ppermute | solution.py:20
  623.0 11.9 collective-permute-start.5
  643.6 521.4 %reduce-scatter.9.cloned.1.call-start = ((), (), s32[]{:S(2)}) async-start(), calls=%async_computation.10 | async-start | bytes 17301504 | tf_op jit(solution)/shard_map/reduce_scatter | solution.py:167
  653.8 876.3 %reduce-scatter.11.cloned.1.call-start = ((), (), s32[]{:S(2)}) async-start(), calls=%async_computation.11 | async-start | bytes 17301504 | tf_op jit(solution)/shard_map/reduce_scatter | solution.py:169
  (40 other events, 724.4 us)
Sparse Core Ops, SparseCore 0:
  9.6 118.5 all-gather.11
  129.7 44.0 all-gather.13
  175.5 148.3 all-gather.15
  325.3 147.8 all-gather.17
  490.9 145.9 reduce-scatter.6
  643.7 154.9 reduce-scatter.4
  801.7 363.2 reduce-scatter.8
  1168.0 362.1 reduce-scatter.10
where the time goes:
time: 1540 us
  waiting for transfers between devices  1130 us (73%)
  blocking collectives  135 us (9%)
  matrix products  114 us (7%)
  starting transfers between devices  90.4 us (6%)
  other arithmetic  24.6 us (2%)
  local copies, waits for them, and re-layouts  24.2 us (2%)
    reduce_scatter x1, waiting for transfers between devices, shards(): lax.psum_scatter(up_w_grad, ('ctx', 'fsdp'), scatter_dimension=0, tiled=T...  366 us
    reduce_scatter x1, waiting for transfers between devices, shards(): lax.psum_scatter(down_w_grad, ('ctx', 'fsdp'), scatter_dimension=0, tiled...  365 us
    all_gather x1, waiting for transfers between devices, shards(): lax.all_gather(down_weight, 'fsdp', axis=0, tiled=True)  143 us
    all_gather x1, waiting for transfers between devices, shards(): lax.all_gather(up_weight, 'fsdp', axis=0, tiled=True)  105 us
    ppermute x14, starting transfers between devices, passed_along(): return lax.ppermute(block, axis, route)  62.4 us
    reduce_scatter x1, waiting for transfers between devices, shards(): lax.psum_scatter(qkv_w_grad, ('ctx', 'fsdp'), scatter_dimension=0, tiled=...  61.1 us
    ppermute x32, waiting for transfers between devices, from_behind(): return lax.ppermute(x, axis, [(i, (i + by) % size) for i in range(size)])  50 us
    unnamed x1, blocking collectives  43.7 us
  transfers between devices with their start and end apart: 54, of which 29 were waited for; matrix products, arithmetic and copies ran while one was open for 9% of the time, Pallas kernels for 0%

commit v1 on v0

--- a/solution.py
+++ b/solution.py
@@ -7,6 +7,25 @@
 HEAD_DIM = 64
 epsilon = 1e-05
 masked_score = -1e30
+
+
+def state_threads(local_values, axis_no):
+    local_values = jnp.moveaxis(local_values, 0, axis_no)
+    tall = local_values.shape
+    return local_values.reshape(
+        *tall[:axis_no], tall[axis_no] * tall[axis_no + 1], *tall[axis_no + 2 :]
+    )
+
+
+def _wrap_positions(out_dim, mesh_dim, my_tile):
+    n_all = lax.axis_size(mesh_dim)
+    entries = [my_tile]
+    pieces_in = [(at, (at + 1) % n_all) for at in range(n_all)]
+    while len(entries) < n_all:
+        entries.append(lax.ppermute(entries[-1], mesh_dim, pieces_in))
+    finding = lax.axis_index(mesh_dim)
+    entries = jnp.stack(entries, 0)[(finding - jnp.arange(n_all)) % n_all]
+    return state_threads(entries, out_dim)
 
 
 def passed_along(block, axis, distance):
@@ -69,7 +88,7 @@
     attn_set = (
         lax.all_gather(norm1_gain, "fsdp", axis=0, tiled=True),
         lax.all_gather(norm1_bias, "fsdp", axis=0, tiled=True),
-        lax.all_gather(qkv_weight, "fsdp", axis=0, tiled=True),
+        _wrap_positions(0, "fsdp", qkv_weight),
         lax.all_gather(qv_bias, "fsdp", axis=0, tiled=True),
         lax.all_gather(out_weight, "fsdp", axis=0, tiled=True),
         lax.all_gather(out_bias, "fsdp", axis=0, tiled=True),

time: 1540 us -> 1520 us (0.987)
  waiting for transfers between devices: 1130 us -> 892 us
  blocking collectives: 135 us -> 302 us
  starting transfers between devices: 90.4 us -> 131 us
    all_gather x1, waiting for transfers between devices: 143 us -> 0.01 us  [shards(): lax.all_gather(down_weight, 'fsdp', axis=0, tiled=True)]
    all_gather x1, waiting for transfers between devices: 105 us -> 0.02 us  [shards(): lax.all_gather(up_weight, 'fsdp', axis=0, tiled=True)]
    all_gather x1, blocking collectives: 8.48 us -> 98.5 us  [shards(): lax.all_gather(norm1_bias, 'fsdp', axis=0, tiled=True)]
    all_gather x1, blocking collectives: 12.6 us -> 86.2 us  [shards(): lax.all_gather(out_bias, 'fsdp', axis=0, tiled=True)]
    ppermute x0 -> x3, waiting for transfers between devices: none -> 61.1 us  [_wrap_positions(): entries.append(lax.ppermute(entries[-1], mesh_dim, pieces_in))]
    all_gather x1 -> x0, waiting for transfers between devices: 34.6 us -> none  [shards(): lax.all_gather(qkv_weight, 'fsdp', axis=0, tiled=True)]
    ppermute x32, starting transfers between devices: 27.6 us -> 53.1 us  [from_behind(): return lax.ppermute(x, axis, [(i, (i + by) % size) for i in range(size)])]
    ppermute x32, waiting for transfers between devices: 50 us -> 31.4 us  [from_behind(): return lax.ppermute(x, axis, [(i, (i + by) % size) for i in range(size)])]
  transfers between devices with their start and end apart: 54 -> 56, of which waited for: 29 -> 26; matrix products, arithmetic and copies ran while one was open for 9% -> 10% of each run, Pallas kernels for 0% -> 0%
where the time goes in v1:
time: 1520 us
  waiting for transfers between devices  892 us (59%)
  blocking collectives  302 us (20%)
  starting transfers between devices  131 us (9%)
  matrix products  114 us (8%)
  other arithmetic  31.2 us (2%)
  local copies, waits for them, and re-layouts  30.6 us (2%)
    reduce_scatter x1, waiting for transfers between devices, shards(): lax.psum_scatter(up_w_grad, ('ctx', 'fsdp'), scatter_dimension=0, tiled=T...  366 us
    reduce_scatter x1, waiting for transfers between devices, shards(): lax.psum_scatter(down_w_grad, ('ctx', 'fsdp'), scatter_dimension=0, tiled...  365 us
    all_gather x1, blocking collectives, shards(): lax.all_gather(norm1_bias, 'fsdp', axis=0, tiled=True)  98.5 us
    all_gather x1, blocking collectives, shards(): lax.all_gather(out_bias, 'fsdp', axis=0, tiled=True)  86.2 us
    ppermute x14, starting transfers between devices, passed_along(): return lax.ppermute(block, axis, route)  64.7 us
    reduce_scatter x1, waiting for transfers between devices, shards(): lax.psum_scatter(qkv_w_grad, ('ctx', 'fsdp'), scatter_dimension=0, tiled=...  62.9 us
    ppermute x3, waiting for transfers between devices, _wrap_positions(): entries.append(lax.ppermute(entries[-1], mesh_dim, pieces_in))  61.1 us
    ppermute x32, starting transfers between devices, from_behind(): return lax.ppermute(x, axis, [(i, (i + by) % size) for i in range(size)])  53.1 us
  transfers between devices with their start and end apart: 56, of which 26 were waited for; matrix products, arithmetic and copies ran while one was open for 10% of the time, Pallas kernels for 0%

profile of v1, /device:TPU:0, one launch (start us, length us, event | category | flops | bytes accessed | tf_op | source)
XLA Modules:
  0.0 1517.0 jit_solution(3306820267182475700)
XLA Ops:
  11.9 61.1 %collective-permute-done.6 = bf16[256,3072]{1,0:T(8,128)(2,1)} collective-permute-done((bf16[256,3072]{1,0:T(8,128)(2,1)S(1)}, bf16[256,3072]{1,0:T(8,128)(2,1)}, u32[]{:S(2)}, u32[]{:S(2)}) %collective-permute-start.6) | collective-permute-done | bytes 1572896 | tf_op jit(solution)/shard_map/ppermute | solution.py:25
  73.0 7.8 collective-permute-start.7
  81.0 86.2 %all-gather.3 = bf16[4,1,256]{2,1,0:T(2,128)(2,1)S(1)} all-gather(bf16[1,1,256]{2,1,0:T(2,128)(2,1)S(1)} %reshape.473), channel_id=1, replica_groups=mesh['ctx'=8,'fsdp'=4] {'fsdp'}, dimensions={0}, use_global_device_ids=true | all-gather | bytes 2560 | tf_op jit(solution)/shard_map/all_gather | solution.py:94
  167.2 21.8 %all-gather.2 = bf16[4,1,512]{2,1,0:T(2,128)(2,1)S(1)} all-gather(bf16[1,1,512]{2,1,0:T(2,128)(2,1)S(1)} %reshape.471), channel_id=1, replica_groups=mesh['ctx'=8,'fsdp'=4] {'fsdp'}, dimensions={0}, use_global_device_ids=true | all-gather | bytes 5120 | tf_op jit(solution)/shard_map/all_gather | solution.py:92
  191.3 98.5 %all-gather.1 = bf16[4,1,256]{2,1,0:T(2,128)(2,1)S(1)} all-gather(bf16[1,1,256]{2,1,0:T(2,128)(2,1)S(1)} %reshape.469), channel_id=1, replica_groups=mesh['ctx'=8,'fsdp'=4] {'fsdp'}, dimensions={0}, use_global_device_ids=true | all-gather | bytes 2560 | tf_op jit(solution)/shard_map/all_gather | solution.py:90
  289.8 7.7 all-gather
  297.7 16.2 %all_gather.41 = bf16[4096]{0:T(1024)(128)(2,1)S(1)} all-gather(bf16[1024]{0:T(1024)(128)(2,1)S(1)} %copy-done.10), channel_id=1, replica_groups=mesh['ctx'=8,'fsdp'=4] {'fsdp'}, dimensions={0}, use_global_device_ids=true | all-gather | bytes 10240 | tf_op jit(solution)/shard_map/all_gather | solution.py:154
  313.9 7.7 all-gather.5
  321.7 10.7 all-gather.4
  333.1 6.6 pad_maximum_fusion
  339.6 6.4 gather_fusion
  354.7 81.5 %while.48 = (s32[]{:T(128)}, bf16[128,16,64]{0,2,1:T(8,128)(2,1)S(1)}, bf16[128,16,64]{0,2,1:T(8,128)(2,1)}, f32[128,16,64]{0,2,1:T(8,128)S(1)}, f32[16,128]{1,0...) while((s32[]{:T(128)}, ...), condition=%wide.region_10.11_spmd.clone, body=%wide.region_6.10_spmd.clone.sunk | while | flops 69264528 | bytes 8294802 | solution.py:141
  356.0 8.5 collective-permute-start.1
  366.9 4.9 collective-permute-start
  378.5 4.9 collective-permute-start
  390.0 4.9 collective-permute-start
  401.5 4.9 collective-permute-start
  413.0 4.9 collective-permute-start
  424.6 4.9 collective-permute-start
  438.8 6.1 convolution_add_fusion
  444.9 7.8 convert_reduce_fusion.2
  462.5 152.0 %while.49 = (s32[]{:T(128)}, bf16[128,16,64]{0,2,1:T(8,128)(2,1)S(1)}, bf16[128,16,64]{0,2,1:T(8,128)(2,1)}, f32[128,16,64]{0,2,1:T(8,128)S(1)}, f32[128,16,64]{...) while((s32[]{:T(128)}, ...), condition=%wide.region_18.19_spmd.clone, body=%wide.region_16.18_spmd.clone.sunk | while | flops 171232400 | bytes 16044550 | solution.py:240
  615.7 6.4 fusion.62
  623.3 8.9 fusion.86
  633.2 10.7 fusion.64
  644.5 7.9 all-gather.6
  652.8 5.5 fusion.87
  659.6 45.0 %all-reduce.8 = (f32[1024]{0:T(1024)S(1)}, f32[1024]{0:T(1024)S(1)}, f32[2048]{0:T(1024)S(1)}, f32[1024]{0:T(1024)S(1)}, f32[1024]{0:T(1024)S(1)}, /*index=5*/f3...) all-reduce(f32[1024]{0:T(1024)S(1)} %get-tuple-element.720, ...), channel_id=2, replica_groups=mesh['ctx'=8,'fsdp'=4] {'ctx','fsdp'}, use_global_device_ids=true, to_apply=%region_22.23.clone | all-reduce | flops 12288 | bytes 98304
  709.3 6.6 fusion.37
  715.8 62.9 %reduce-scatter.5.cloned.1.call-done = f32[32,3072]{1,0:T(8,128)} async-done(((f32[1024,3072]{1,0:T(8,128)}), f32[32,3072]{1,0:T(8,128)}) %reduce-scatter.5.cloned.1.call-update) | async-done | bytes 393232 | tf_op jit(solution)/shard_map/reduce_scatter | solution.py:264
  778.8 366.2 %reduce-scatter.9.cloned.1.call-done = f32[32,4096]{1,0:T(8,128)} async-done(((f32[1024,4096]{1,0:T(8,128)}), f32[32,4096]{1,0:T(8,128)}) %reduce-scatter.9.cloned.1.call-update) | async-done | bytes 524304 | tf_op jit(solution)/shard_map/reduce_scatter | solution.py:186
  1144.9 365.2 %reduce-scatter.11.cloned.1.call-done = f32[128,1024]{1,0:T(8,128)} async-done(((f32[4096,1024]{1,0:T(8,128)}), f32[128,1024]{1,0:T(8,128)}) %reduce-scatter.11.cloned.1.call-update) | async-done | bytes 524304 | tf_op jit(solution)/shard_map/reduce_scatter | solution.py:188
  (410 shorter events, 232.8 us)
Async XLA Ops:
  7.2 429.2 %all-gather.11.cloned.1.call-start = ((), (), s32[]{:S(2)}) async-start(), calls=%async_computation.4 | async-start | bytes 2621440 | tf_op jit(solution)/shard_map/all_gather | solution.py:93
  8.0 430.7 %all-gather.13.cloned.1.call-start = ((), (), s32[]{:S(2)}) async-start(), calls=%async_computation.5 | async-start | bytes 10485760 | tf_op jit(solution)/shard_map/all_gather | solution.py:153
  8.8 436.1 %all-gather.15.cloned.1.call-start = ((), (), s32[]{:S(2)}) async-start(), calls=%async_computation.6 | async-start | bytes 10485760 | tf_op jit(solution)/shard_map/all_gather | solution.py:155
  8.8 64.2 %collective-permute-start.6 = (bf16[256,3072]{1,0:T(8,128)(2,1)S(1)}, bf16[256,3072]{1,0:T(8,128)(2,1)}, u32[]{:S(2)}, u32[]{:S(2)}) collective-permute-start(bf16[256,3072]{1,0:T(8,128)(2,1)S(1)} %copy-done.9), channel_id=1, source_target_pairs={{0,1},{1,2},{2,3},{3,0},{4,5},{5,6},{6,7},{7,4},{8,9},{9,10},{10,1... | collective-permute-start | bytes 4718600 | tf_op jit(solution)/shard_map/ppermute | solution.py:25
  73.0 116.0 %collective-permute-start.7 = (bf16[256,3072]{1,0:T(8,128)(2,1)}, bf16[256,3072]{1,0:T(8,128)(2,1)}, u32[]{:S(2)}, u32[]{:S(2)}) collective-permute-start(bf16[256,3072]{1,0:T(8,128)(2,1)} %collective-permute-done.6), channel_id=1, source_target_pairs={{0,1},{1,2},{2,3},{3,0},{4,5},{5,6},{6,7},{7,4},{8,9},{9,10},{10,1... | collective-permute-start | bytes 4718600 | tf_op jit(solution)/shard_map/ppermute | solution.py:25
  80.9 635.0 %reduce-scatter.7.cloned.1.call-start = ((), (), s32[]{:S(2)}) async-start(), calls=%async_computation.8 | async-start | bytes 4325376 | tf_op jit(solution)/shard_map/reduce_scatter | solution.py:266
  189.0 144.1 %collective-permute-start.8 = (bf16[256,3072]{1,0:T(8,128)(2,1)}, bf16[256,3072]{1,0:T(8,128)(2,1)}, u32[]{:S(2)}, u32[]{:S(2)}) collective-permute-start(bf16[256,3072]{1,0:T(8,128)(2,1)} %collective-permute-done.7), channel_id=1, source_target_pairs={{0,1},{1,2},{2,3},{3,0},{4,5},{5,6},{6,7},{7,4},{8,9},{9,10},{10,1... | collective-permute-start | bytes 4718600 | tf_op jit(solution)/shard_map/ppermute | solution.py:25
  462.4 316.3 %reduce-scatter.5.cloned.1.call-start = ((), (), s32[]{:S(2)}) async-start(), calls=%async_computation.7 | async-start | bytes 12976128 | tf_op jit(solution)/shard_map/reduce_scatter | solution.py:264
  462.8 20.4 %collective-permute-start.2 = (bf16[128,16,64]{0,2,1:T(8,128)(2,1)S(1)}, bf16[128,16,64]{0,2,1:T(8,128)(2,1)S(1)}, u32[]{:S(2)}, u32[]{:S(2)}) collective-permute-start(bf16[128,16,64]{0,2,1:T(8,128)(2,1)S(1)} %copy.89), channel_id=1, source_target_pairs={{0,4},{4,8},{8,12},{12,16},{16,20},{20,24},{24,28},{28,0},{1,5},{5... | collective-permute-start | bytes 786440 | tf_op jit(solution)/shard_map/while/body/eval_jaxpr/ppermute | solution.py:39
  467.3 15.8 %collective-permute-start.3 = (bf16[128,16,64]{0,2,1:T(8,128)(2,1)S(1)}, bf16[128,16,64]{0,2,1:T(8,128)(2,1)}, u32[]{:S(2)}, u32[]{:S(2)}) collective-permute-start(bf16[128,16,64]{0,2,1:T(8,128)(2,1)S(1)} %copy.90), channel_id=1, source_target_pairs={{0,4},{4,8},{8,12},{12,16},{16,20},{20,24},{24,28},{28,0},{1,5},{5... | collective-permute-start | bytes 786440 | tf_op jit(solution)/shard_map/while/body/eval_jaxpr/ppermute | solution.py:39
  483.2 20.0 %collective-permute-start.2 = (bf16[128,16,64]{0,2,1:T(8,128)(2,1)S(1)}, bf16[128,16,64]{0,2,1:T(8,128)(2,1)S(1)}, u32[]{:S(2)}, u32[]{:S(2)}) collective-permute-start(bf16[128,16,64]{0,2,1:T(8,128)(2,1)S(1)} %copy.89), channel_id=1, source_target_pairs={{0,4},{4,8},{8,12},{12,16},{16,20},{20,24},{24,28},{28,0},{1,5},{5... | collective-permute-start | bytes 786440 | tf_op jit(solution)/shard_map/while/body/eval_jaxpr/ppermute | solution.py:39
  486.7 16.4 %collective-permute-start.3 = (bf16[128,16,64]{0,2,1:T(8,128)(2,1)S(1)}, bf16[128,16,64]{0,2,1:T(8,128)(2,1)}, u32[]{:S(2)}, u32[]{:S(2)}) collective-permute-start(bf16[128,16,64]{0,2,1:T(8,128)(2,1)S(1)} %copy.90), channel_id=1, source_target_pairs={{0,4},{4,8},{8,12},{12,16},{16,20},{20,24},{24,28},{28,0},{1,5},{5... | collective-permute-start | bytes 786440 | tf_op jit(solution)/shard_map/while/body/eval_jaxpr/ppermute | solution.py:39
  503.2 18.7 %collective-permute-start.2 = (bf16[128,16,64]{0,2,1:T(8,128)(2,1)S(1)}, bf16[128,16,64]{0,2,1:T(8,128)(2,1)S(1)}, u32[]{:S(2)}, u32[]{:S(2)}) collective-permute-start(bf16[128,16,64]{0,2,1:T(8,128)(2,1)S(1)} %copy.89), channel_id=1, source_target_pairs={{0,4},{4,8},{8,12},{12,16},{16,20},{20,24},{24,28},{28,0},{1,5},{5... | collective-permute-start | bytes 786440 | tf_op jit(solution)/shard_map/while/body/eval_jaxpr/ppermute | solution.py:39
  504.3 17.7 %collective-permute-start.3 = (bf16[128,16,64]{0,2,1:T(8,128)(2,1)S(1)}, bf16[128,16,64]{0,2,1:T(8,128)(2,1)}, u32[]{:S(2)}, u32[]{:S(2)}) collective-permute-start(bf16[128,16,64]{0,2,1:T(8,128)(2,1)S(1)} %copy.90), channel_id=1, source_target_pairs={{0,4},{4,8},{8,12},{12,16},{16,20},{20,24},{24,28},{28,0},{1,5},{5... | collective-permute-start | bytes 786440 | tf_op jit(solution)/shard_map/while/body/eval_jaxpr/ppermute | solution.py:39
  510.6 10.4 collective-permute-start.5
  522.0 18.6 %collective-permute-start.2 = (bf16[128,16,64]{0,2,1:T(8,128)(2,1)S(1)}, bf16[128,16,64]{0,2,1:T(8,128)(2,1)S(1)}, u32[]{:S(2)}, u32[]{:S(2)}) collective-permute-start(bf16[128,16,64]{0,2,1:T(8,128)(2,1)S(1)} %copy.89), channel_id=1, source_target_pairs={{0,4},{4,8},{8,12},{12,16},{16,20},{20,24},{24,28},{28,0},{1,5},{5... | collective-permute-start | bytes 786440 | tf_op jit(solution)/shard_map/while/body/eval_jaxpr/ppermute | solution.py:39
  523.1 17.5 %collective-permute-start.3 = (bf16[128,16,64]{0,2,1:T(8,128)(2,1)S(1)}, bf16[128,16,64]{0,2,1:T(8,128)(2,1)}, u32[]{:S(2)}, u32[]{:S(2)}) collective-permute-start(bf16[128,16,64]{0,2,1:T(8,128)(2,1)S(1)} %copy.90), channel_id=1, source_target_pairs={{0,4},{4,8},{8,12},{12,16},{16,20},{20,24},{24,28},{28,0},{1,5},{5... | collective-permute-start | bytes 786440 | tf_op jit(solution)/shard_map/while/body/eval_jaxpr/ppermute | solution.py:39
  528.9 10.7 collective-permute-start.5
  540.6 18.4 %collective-permute-start.2 = (bf16[128,16,64]{0,2,1:T(8,128)(2,1)S(1)}, bf16[128,16,64]{0,2,1:T(8,128)(2,1)S(1)}, u32[]{:S(2)}, u32[]{:S(2)}) collective-permute-start(bf16[128,16,64]{0,2,1:T(8,128)(2,1)S(1)} %copy.89), channel_id=1, source_target_pairs={{0,4},{4,8},{8,12},{12,16},{16,20},{20,24},{24,28},{28,0},{1,5},{5... | collective-permute-start | bytes 786440 | tf_op jit(solution)/shard_map/while/body/eval_jaxpr/ppermute | solution.py:39
  541.7 17.4 %collective-permute-start.3 = (bf16[128,16,64]{0,2,1:T(8,128)(2,1)S(1)}, bf16[128,16,64]{0,2,1:T(8,128)(2,1)}, u32[]{:S(2)}, u32[]{:S(2)}) collective-permute-start(bf16[128,16,64]{0,2,1:T(8,128)(2,1)S(1)} %copy.90), channel_id=1, source_target_pairs={{0,4},{4,8},{8,12},{12,16},{16,20},{20,24},{24,28},{28,0},{1,5},{5... | collective-permute-start | bytes 786440 | tf_op jit(solution)/shard_map/while/body/eval_jaxpr/ppermute | solution.py:39
  547.2 10.9 collective-permute-start.5
  559.1 18.4 %collective-permute-start.2 = (bf16[128,16,64]{0,2,1:T(8,128)(2,1)S(1)}, bf16[128,16,64]{0,2,1:T(8,128)(2,1)S(1)}, u32[]{:S(2)}, u32[]{:S(2)}) collective-permute-start(bf16[128,16,64]{0,2,1:T(8,128)(2,1)S(1)} %copy.89), channel_id=1, source_target_pairs={{0,4},{4,8},{8,12},{12,16},{16,20},{20,24},{24,28},{28,0},{1,5},{5... | collective-permute-start | bytes 786440 | tf_op jit(solution)/shard_map/while/body/eval_jaxpr/ppermute | solution.py:39
  560.2 17.4 %collective-permute-start.3 = (bf16[128,16,64]{0,2,1:T(8,128)(2,1)S(1)}, bf16[128,16,64]{0,2,1:T(8,128)(2,1)}, u32[]{:S(2)}, u32[]{:S(2)}) collective-permute-start(bf16[128,16,64]{0,2,1:T(8,128)(2,1)S(1)} %copy.90), channel_id=1, source_target_pairs={{0,4},{4,8},{8,12},{12,16},{16,20},{20,24},{24,28},{28,0},{1,5},{5... | collective-permute-start | bytes 786440 | tf_op jit(solution)/shard_map/while/body/eval_jaxpr/ppermute | solution.py:39
  565.4 11.1 collective-permute-start.5
  577.6 18.4 %collective-permute-start.2 = (bf16[128,16,64]{0,2,1:T(8,128)(2,1)S(1)}, bf16[128,16,64]{0,2,1:T(8,128)(2,1)S(1)}, u32[]{:S(2)}, u32[]{:S(2)}) collective-permute-start(bf16[128,16,64]{0,2,1:T(8,128)(2,1)S(1)} %copy.89), channel_id=1, source_target_pairs={{0,4},{4,8},{8,12},{12,16},{16,20},{20,24},{24,28},{28,0},{1,5},{5... | collective-permute-start | bytes 786440 | tf_op jit(solution)/shard_map/while/body/eval_jaxpr/ppermute | solution.py:39
  578.6 17.4 %collective-permute-start.3 = (bf16[128,16,64]{0,2,1:T(8,128)(2,1)S(1)}, bf16[128,16,64]{0,2,1:T(8,128)(2,1)}, u32[]{:S(2)}, u32[]{:S(2)}) collective-permute-start(bf16[128,16,64]{0,2,1:T(8,128)(2,1)S(1)} %copy.90), channel_id=1, source_target_pairs={{0,4},{4,8},{8,12},{12,16},{16,20},{20,24},{24,28},{28,0},{1,5},{5... | collective-permute-start | bytes 786440 | tf_op jit(solution)/shard_map/while/body/eval_jaxpr/ppermute | solution.py:39
  583.6 11.3 collective-permute-start.5
  596.0 18.4 %collective-permute-start.2 = (bf16[128,16,64]{0,2,1:T(8,128)(2,1)S(1)}, bf16[128,16,64]{0,2,1:T(8,128)(2,1)S(1)}, u32[]{:S(2)}, u32[]{:S(2)}) collective-permute-start(bf16[128,16,64]{0,2,1:T(8,128)(2,1)S(1)} %copy.89), channel_id=1, source_target_pairs={{0,4},{4,8},{8,12},{12,16},{16,20},{20,24},{24,28},{28,0},{1,5},{5... | collective-permute-start | bytes 786440 | tf_op jit(solution)/shard_map/while/body/eval_jaxpr/ppermute | solution.py:39
  597.1 17.4 %collective-permute-start.3 = (bf16[128,16,64]{0,2,1:T(8,128)(2,1)S(1)}, bf16[128,16,64]{0,2,1:T(8,128)(2,1)}, u32[]{:S(2)}, u32[]{:S(2)}) collective-permute-start(bf16[128,16,64]{0,2,1:T(8,128)(2,1)S(1)} %copy.90), channel_id=1, source_target_pairs={{0,4},{4,8},{8,12},{12,16},{16,20},{20,24},{24,28},{28,0},{1,5},{5... | collective-permute-start | bytes 786440 | tf_op jit(solution)/shard_map/while/body/eval_jaxpr/ppermute | solution.py:39
  601.9 11.6 collective-permute-start.5
  622.1 522.8 %reduce-scatter.9.cloned.1.call-start = ((), (), s32[]{:S(2)}) async-start(), calls=%async_computation.9 | async-start | bytes 17301504 | tf_op jit(solution)/shard_map/reduce_scatter | solution.py:186
  632.2 877.9 %reduce-scatter.11.cloned.1.call-start = ((), (), s32[]{:S(2)}) async-start(), calls=%async_computation.10 | async-start | bytes 17301504 | tf_op jit(solution)/shard_map/reduce_scatter | solution.py:188
  (43 other events, 2446.2 us)
Sparse Core Ops, SparseCore 0:
  9.6 72.8 all-gather.10
  84.1 202.8 all-gather.12
  288.5 148.8 all-gather.14
  462.6 154.8 reduce-scatter.6
  623.9 154.7 reduce-scatter.4
  781.6 363.3 reduce-scatter.8
  1147.9 362.1 reduce-scatter.10
